TPU v7x, 128 devices: a whole 4x4x4 slice. The times are simulated.
128 devices in a mesh: rcpt: 8 (over x, y_hi), space: 16 (over z, y_lo, core).
Axes of the slice: x: 4, y: 4 (y_hi: 2, y_lo: 2; y = y_hi * 2 + y_lo), z: 4, core: 2. Of those that a mesh axis runs over, the one named last changes fastest.
Arguments:
- adjoint_end: float32 [64, 4, 512, 1024], P('rcpt', None, 'space'), may hold values from -6 to 6
- currents: bfloat16 [8, 2, 4, 512, 1024], P('rcpt', None, None, 'space'), may hold values from -0.29882812 to 0.29882812
- plan: int32 [4], replicated, may hold values from 0 to 7, as said below
- water_mask: int32 [512, 1024], P('space'), may hold values 0 or 1
- mixing: float32 [3, 512, 1024], P(None, 'space'), may hold values from 0.02 to 0.2
- decay: float32 [64], P('rcpt'), may hold values from 0.02 to 0.5
- obs_weight: float32 [4, 64], P(None, 'rcpt'), may hold values from 0.3 to 3
- release_cells: int32 [16, 128, 128], P('space'), may hold values from 0 to 32767
- profiles: float32 [16, 128, 512, 128], P(None, ('rcpt', 'space')), may hold values from -0.25 to 0.25
Outputs:
- adjoint_start: float32 [64, 4, 512, 1024], P('rcpt', None, 'space')
- sensitivity: float32 [16, 128, 64, 128], P(None, ('rcpt', 'space'))
Inputs may be any that keep to these rules, and one draw needn't show every extreme that they name: 4 distinct store slots; hour h's currents are currents[plan[h]], held by rcpt index plan[h].
All inputs are finite; a program needn't handle non-finite values. No bound on the sum of `water_mask` on one device may be relied on, other than what follows from the above.
Results may differ from a plain program's by a relative error of at most 0.0003.
Values may be sent and summed in bfloat16 or wider, within the bound.
No kernel may reach another device: no remote copies, remote signals or barrier semaphores. Data moves between devices by JAX's collectives and lax.ppermute only.
A program may use at most 256 MiB of HBM per device.

v0:
```python
import jax
import jax.numpy as jnp
from jax import lax
from jax.sharding import PartitionSpec as P

HOURS = 4


diffusion_number = 0.08


def broadcast(value, axis, source):
    kept = jnp.where(lax.axis_index(axis) == source, value, 0).astype(value.dtype)
    return lax.psum(kept, axis)


def with_halo(block, sides, width):
    for axis, dim in sides:
        count = lax.axis_size(axis)
        forward = [(i, i + 1) for i in range(count - 1)]
        backward = [(target, source) for source, target in forward]
        low = lax.ppermute(
            lax.slice_in_dim(block, block.shape[dim] - width, None, axis=dim), axis, forward
        )
        high = lax.ppermute(lax.slice_in_dim(block, 0, width, axis=dim), axis, backward)
        block = jnp.concatenate([low, block, high], axis=dim)
    return block


def next_column(values):
    edge = jnp.zeros_like(values[..., :1])
    return jnp.concatenate([values[..., 1:], edge], -1)


def prev_column(values):
    edge = jnp.zeros_like(values[..., :1])
    return jnp.concatenate([edge, values[..., :-1]], -1)


def transport(extended, water, current, mixing):
    center = extended[:, :, 1:-1]
    along = current[0].astype(jnp.float32)
    across = current[1].astype(jnp.float32)
    inner = water[1:-1]
    weight_down = (jax.nn.relu(along) + diffusion_number) * water[2:]
    weight_up = (jax.nn.relu(-along) + diffusion_number) * water[:-2]
    weight_right = (jax.nn.relu(across) + diffusion_number) * next_column(inner)
    weight_left = (jax.nn.relu(-across) + diffusion_number) * prev_column(inner)
    moved = center + weight_down * (extended[:, :, 2:] - center)
    moved = moved + weight_up * (extended[:, :, :-2] - center)
    moved = moved + weight_right * (next_column(center) - center)
    moved = moved + weight_left * (prev_column(center) - center)
    moved = moved * inner
    vertical_flux = mixing * (moved[:, 1:] - moved[:, :-1])
    zeros = jnp.zeros_like(moved[:, :1])
    return (
        moved
        + jnp.concatenate([vertical_flux, zeros], 1)
        - jnp.concatenate([zeros, vertical_flux], 1)
    )


def on_device(
    adjoint_end, currents, plan, water_mask, mixing, decay, obs_weight, release_cells, profiles
):
    slot_count = currents.shape[0]
    own_rows = adjoint_end.shape[2]
    keep = (1.0 - decay)[:, None, None, None]
    hourly = []
    for hour_index in range(HOURS):
        slot_id = plan[hour_index]
        holder = slot_id // slot_count
        mine = lax.dynamic_index_in_dim(currents, slot_id % slot_count, 0, keepdims=False)
        hourly.append(broadcast(mine, "rcpt", holder))
    rim_mask = with_halo(water_mask, (("space", 0),), 1)
    water = rim_mask.astype(jnp.float32)
    inner = water[1:-1]
    source = inner * adjoint_end
    field = adjoint_end
    for hour_index in reversed(range(HOURS)):
        extended = with_halo(field, (("space", 2),), 1)
        mixed = transport(extended, water, hourly[hour_index], mixing)
        field = keep * mixed + obs_weight[hour_index][:, None, None, None] * source
    local_recv = field.shape[0]
    levels = field.shape[1]
    width = field.shape[3]
    block_count = release_cells.shape[1]
    block_cells = release_cells.shape[2]
    strip_cells = own_rows * width
    flat = field.reshape(local_recv, levels * strip_cells)
    level_start = jnp.arange(levels, dtype=jnp.int32) * strip_cells
    positions = level_start[None, :, None] + release_cells[0][:, None, :]
    picked = jnp.take(flat, positions.reshape(-1), axis=1)
    picked = picked.reshape(local_recv, block_count, levels * block_cells)
    picked = jnp.transpose(picked, (1, 0, 2))
    batches = lax.axis_size("rcpt")
    strips = lax.axis_size("space")
    sample_len = levels * block_cells
    sending = picked.reshape(1, block_count, local_recv, sample_len)
    gathered = lax.all_to_all(sending, ("rcpt", "space"), split_axis=1, concat_axis=0, tiled=True)
    own_blocks = gathered.shape[1]
    gathered = gathered.reshape(batches, strips, own_blocks, local_recv, sample_len)
    gathered = jnp.transpose(gathered, (1, 2, 0, 3, 4))
    gathered = gathered.reshape(strips, own_blocks, batches * local_recv, sample_len)
    result = jnp.einsum("sbmk,sbkp->sbmp", gathered, profiles, precision=lax.Precision.HIGHEST)
    return (field, result)


def solution(mesh):
    placed = (
        P("rcpt", None, "space", None),
        P("rcpt", None, None, "space", None),
        P(),
        P("space", None),
        P(None, "space", None),
        P("rcpt"),
        P(None, "rcpt"),
        P("space", None, None),
        P(None, ("rcpt", "space"), None, None),
    )
    return jax.shard_map(
        on_device,
        mesh=mesh,
        in_specs=placed,
        out_specs=(P("rcpt", None, "space", None), P(None, ("rcpt", "space"), None, None)),
        check_vma=False,
    )
```

profile of v0, /device:TPU:1, one launch (start us, length us, event | category | flops | bytes accessed | tf_op | source)
XLA Modules:
  0.0 1283.8 jit_solution(15236937972959559625)
XLA Ops:
  8.0 4.6 collective-permute-start
  14.7 4.6 copy.20
  23.2 3.8 collective-permute-start.3
  31.7 8.1 fusion.111
  41.5 101.4 %all-reduce.21.cloned.1.call-done = (bf16[2,4,32,1024]{3,2,1,0:T(8,128)(2,1)}, bf16[2,4,32,1024]{3,2,1,0:T(8,128)(2,1)}, bf16[2,4,32,1024]{3,2,1,0:T(8,128)(2,1)}, bf16[2,4,32,1024]{3,2,1,0:T(8,128)(2,1)}) async-done(((bf16[2,4,32,1024]{3,2,1,0:T(8,128)(2,1)}, bf16[2,4,32,1024]{3,2,1,0:T(8,128)(2,1)}, bf16[2,4,32,1024]{3,2,1,0:T(8,128)(2,1)}, bf16[2,4,32,1024]{3,2,1,0:T(8,128)(2,1)}), ...) | async-done | bytes 2097168 | tf_op jit(solution)/shard_map/psum | solution.py:14
  144.3 9.5 fusion.32
  159.5 4.9 fusion.109
  164.4 5.8 collective-permute-start.4
  174.9 7.2 fusion.23
  182.9 3.4 multiply_add_fusion.2
  188.8 3.5 collective-permute-start.7
  192.4 4.9 fusion.107
  197.3 7.2 fusion.14
  210.8 4.2 collective-permute-start.9
  215.0 4.9 fusion.105
  220.0 7.2 fusion.5
  228.1 5.3 multiply_add_fusion
  233.4 30.4 %copy.29 = f32[8,4,32,1024]{0,3,2,1:T(8,128)} copy(f32[8,4,32,1024]{3,0,2,1:T(8,128)} %multiply_add_fusion) | data formatting | bytes 8388608 | tf_op jit(solution)/shard_map/add | solution.py:83
  263.8 948.6 %gather_fusion = f32[65536,8]{1,0:T(8,128)} fusion(f32[8,131072]{0,1:T(8,128)} %bitcast.30, s32[65536]{0:T(1024)S(1)} %copy-done.18), kind=kCustom, calls=%fused_computation | custom fusion | bytes 4456448 | tf_op jit(solution)/shard_map/jit(_take)/gather | solution.py:93
  1212.5 17.7 %copy.30 = f32[8,128,512]{2,0,1:T(8,128)S(1)} copy(f32[8,128,512]{0,2,1:T(8,128)} %bitcast.89) | data formatting | bytes 4194304 | tf_op jit(solution)/shard_map/jit(_take)/gather | solution.py:93
  1231.8 9.5 all-to-all-start
  1241.3 6.6 copy.32
  1247.9 23.2 %all-to-all-done = f32[1,128,8,512]{3,2,0,1:T(8,128)S(1)} async-done(((f32[1,128,8,512]{3,2,0,1:T(8,128)}), f32[1,128,8,512]{3,2,0,1:T(8,128)S(1)}, u32[]{:S(2)}, u32[]{:S(2)}) %all-to-all-start) | async-done | bytes 2097184 | tf_op jit(solution)/shard_map/all_to_all | solution.py:100
  1271.1 5.6 fusion.44
  (103 shorter events, 34.1 us)
Async XLA Ops:
  7.2 135.7 %all-reduce.21.cloned.1.call-start = ((), (), s32[]{:S(2)}) async-start(), calls=%async_computation.1 | async-start | bytes 4194304 | tf_op jit(solution)/shard_map/psum | solution.py:14
  8.0 33.2 %collective-permute-start = (s32[1,1024]{1,0:T(1,128)S(1)}, s32[1,1024]{1,0:T(1,128)S(1)}, u32[]{:S(2)}, u32[]{:S(2)}) collective-permute-start(s32[1,1024]{1,0:T(1,128)S(1)} %get-tuple-element.65), channel_id=1, source_target_pairs={{0,1},{1,2},{2,3},{3,4},{4,5},{5,6},{6,7},{7,8},{8,9},{9,10},{10,1... | collective-permute-start | bytes 12296 | tf_op jit(solution)/shard_map/ppermute | solution.py:22
  12.6 14.5 %copy-start.25 = (s32[4]{0:T(128)S(1)}, s32[4]{0:T(128)}, u32[]{:S(2)}) copy-start(s32[4]{0:T(128)} %param.11) | copy-start | bytes 52
  12.6 17.7 %copy-start.22 = (bf16[1,2,4,32,1024]{4,3,2,1,0:T(8,128)(2,1)S(1)}, bf16[1,2,4,32,1024]{4,3,2,1,0:T(8,128)(2,1)}, u32[]{:S(2)}) copy-start(bf16[1,2,4,32,1024]{4,3,2,1,0:T(8,128)(2,1)} %param.10) | copy-start | bytes 1572868
  12.6 28.6 %collective-permute-start.1 = (s32[1,1024]{1,0:T(1,128)S(1)}, s32[1,1024]{1,0:T(1,128)S(1)}, u32[]{:S(2)}, u32[]{:S(2)}) collective-permute-start(s32[1,1024]{1,0:T(1,128)S(1)} %get-tuple-element.66), channel_id=1, source_target_pairs={{1,0},{2,1},{3,2},{4,3},{5,4},{6,5},{7,6},{8,7},{9,8},{10,9},{11,1... | collective-permute-start | bytes 12296 | tf_op jit(solution)/shard_map/ppermute | solution.py:25
  21.3 122.9 %collective-permute-start.2 = (f32[8,4,1,1024]{3,0,2,1:T(8,128)S(1)}, f32[8,4,1,1024]{3,0,2,1:T(8,128)S(1)}, u32[]{:S(2)}, u32[]{:S(2)}) collective-permute-start(f32[8,4,1,1024]{3,0,2,1:T(8,128)S(1)} %get-tuple-element.26), channel_id=1, source_target_pairs={{1,0},{2,1},{3,2},{4,3},{5,4},{6,5},{7,6},{8,7},{9,8},{10,9},{11,1... | collective-permute-start | bytes 393224 | tf_op jit(solution)/shard_map/ppermute | solution.py:25
  23.2 121.0 %collective-permute-start.3 = (f32[8,4,1,1024]{3,0,2,1:T(8,128)S(1)}, f32[8,4,1,1024]{3,0,2,1:T(8,128)S(1)}, u32[]{:S(2)}, u32[]{:S(2)}) collective-permute-start(f32[8,4,1,1024]{3,0,2,1:T(8,128)S(1)} %get-tuple-element.27), channel_id=1, source_target_pairs={{0,1},{1,2},{2,3},{3,4},{4,5},{5,6},{6,7},{7,8},{8,9},{9,10},{10,1... | collective-permute-start | bytes 393224 | tf_op jit(solution)/shard_map/ppermute | solution.py:22
  31.7 9.5 copy-start.24
  41.5 102.8 %copy-start.14 = (f32[32,1024]{1,0:T(8,128)}, f32[32,1024]{1,0:T(8,128)S(1)}, u32[]{:S(2)}) copy-start(f32[32,1024]{1,0:T(8,128)S(1)} %get-tuple-element.60) | copy-start | bytes 393220
  41.5 102.8 %copy-start.16 = (f32[32,1024]{1,0:T(8,128)}, f32[32,1024]{1,0:T(8,128)S(1)}, u32[]{:S(2)}) copy-start(f32[32,1024]{1,0:T(8,128)S(1)} %get-tuple-element.62) | copy-start | bytes 393220
  144.3 9.5 copy-start.2
  159.4 12.9 %copy-start.15 = (f32[32,1024]{1,0:T(8,128)S(1)}, f32[32,1024]{1,0:T(8,128)}, u32[]{:S(2)}) copy-start(f32[32,1024]{1,0:T(8,128)} %copy-done.14) | copy-start | bytes 393220
  159.4 12.9 %copy-start.17 = (f32[32,1024]{1,0:T(8,128)S(1)}, f32[32,1024]{1,0:T(8,128)}, u32[]{:S(2)}) copy-start(f32[32,1024]{1,0:T(8,128)} %copy-done.16) | copy-start | bytes 393220
  159.4 12.9 %copy-start.19 = (bf16[2,4,32,1024]{3,2,1,0:T(8,128)(2,1)S(1)}, bf16[2,4,32,1024]{3,2,1,0:T(8,128)(2,1)}, u32[]{:S(2)}) copy-start(bf16[2,4,32,1024]{3,2,1,0:T(8,128)(2,1)} %get-tuple-element.9) | copy-start | bytes 1572868
  159.4 12.9 %copy-start.20 = (bf16[2,4,32,1024]{3,2,1,0:T(8,128)(2,1)S(1)}, bf16[2,4,32,1024]{3,2,1,0:T(8,128)(2,1)}, u32[]{:S(2)}) copy-start(bf16[2,4,32,1024]{3,2,1,0:T(8,128)(2,1)} %get-tuple-element.10) | copy-start | bytes 1572868
  159.4 12.9 %copy-start.21 = (bf16[2,4,32,1024]{3,2,1,0:T(8,128)(2,1)S(1)}, bf16[2,4,32,1024]{3,2,1,0:T(8,128)(2,1)}, u32[]{:S(2)}) copy-start(bf16[2,4,32,1024]{3,2,1,0:T(8,128)(2,1)} %get-tuple-element.11) | copy-start | bytes 1572868
  164.4 10.5 collective-permute-start.4
  170.2 4.7 collective-permute-start.5
  186.4 10.9 collective-permute-start.6
  188.8 8.5 collective-permute-start.7
  208.8 11.1 collective-permute-start.8
  210.8 9.2 collective-permute-start.9
  233.4 30.5 %copy-start.18 = (s32[65536]{0:T(1024)S(1)}, s32[65536]{0:T(1024)}, u32[]{:S(2)}) copy-start(s32[65536]{0:T(1024)} %broadcast_clamp_fusion) | copy-start | bytes 786436
  1231.8 39.3 %all-to-all-start = ((f32[1,128,8,512]{3,2,0,1:T(8,128)}), f32[1,128,8,512]{3,2,0,1:T(8,128)S(1)}, u32[]{:S(2)}, u32[]{:S(2)}) async-start(f32[1,128,8,512]{3,2,0,1:T(8,128)} %select_bitcast_fusion), calls=%async_computation | async-start | bytes 4194304 | tf_op jit(solution)/shard_map/all_to_all | solution.py:100
  (16 other events, 122.6 us)
Sparse Core Ops, SparseCore 0:
  31.8 111.0 all-reduce.20
where the time goes:
time: 1300 us; the launch traced here: 1280 us
  local copies, waits for them, and re-layouts  1040 us (80%)
  waiting for transfers between devices  125 us (10%)
  other arithmetic  58 us (4%)
  starting transfers between devices  41.9 us (3%)
  between operations  17.4 us (1%)
    gather x2, local copies, waits for them, and re-layouts, on_device(): picked = jnp.take(flat, positions.reshape(-1), axis=1)  966 us
    psum x1, waiting for transfers between devices, broadcast(): return lax.psum(kept, axis)  101 us
    mul x4, other arithmetic, transport(): moved = moved * inner  31.1 us
    add x1, local copies, waits for them, and re-layouts, on_device(): field = keep * mixed + obs_weight[hour_index][:, None, None, None] * source  30.4 us
  transfers between devices with their start and end apart: 12, of which 2 were waited for; matrix products, arithmetic and copies ran while one was open for 3% of the time, Pallas kernels for 0%

commit v1 on v0

v1 whole, which is shorter than its diff:
```python
import functools

import jax
import jax.numpy as jnp
from jax import lax
from jax.experimental import pallas as pl
from jax.experimental.pallas import tpu as pltpu
from jax.sharding import PartitionSpec as P

HOURS = 4
RIM = 4
LANES = 128


diffusion_number = 0.08


def transport_kernel(
    where_ref, cells_ref, keep_ref, obs_ref, adj_hbm, rim_hbm, water_hbm, mix_hbm,
    p0, p1, p2, p3, p4, p5, p6, p7,
    start_hbm, samples_hbm,
    strips, rims, field, source, water_in, water, masks, mix, cur, weights, table, picked, outgoing,
    sem_adj, sem_rim, sem_water, sem_mix, sem_cur, sem_out, sem_samples,
):
    levels, slots = field.shape[1], field.shape[2]
    tiles = strips.shape[0]
    own = slots - 2 * RIM
    recv = field.shape[3]
    x_here = where_ref[0]
    y_here = where_ref[1]

    copies = []
    for j in range(tiles):
        lanes = pl.ds(j * LANES, LANES)
        copies.append(pltpu.make_async_copy(adj_hbm.at[:, lanes], strips.at[j], sem_adj))
        copies.append(pltpu.make_async_copy(rim_hbm.at[:, lanes], rims.at[j], sem_rim))
    water_copy = pltpu.make_async_copy(water_hbm, water_in, sem_water)
    for j in range(tiles):
        lanes = pl.ds(j * LANES, LANES)
        copies.append(pltpu.make_async_copy(mix_hbm.at[:, :, lanes], mix.at[:, j, pl.ds(0, own)], sem_mix))
    for copy in copies:
        copy.start()
    water_copy.start()
    cur_copies = []
    for order, piece in enumerate((p0, p1, p2, p3, p4, p5, p6, p7)):
        dx, dy = order // 2, order % 2
        to = lax.rem(x_here + dx, 4) * 2 + (y_here + dy - 2 * y_here * dy)
        cur_copies.append(pltpu.make_async_copy(piece, cur.at[to], sem_cur))
    for copy in cur_copies:
        copy.start()
    for copy in copies:
        copy.wait()
    water_copy.wait()

    lane = lax.broadcasted_iota(jnp.int32, (8, LANES), 1)
    first = lane == 0
    last = lane == LANES - 1

    rim_first = levels * recv * 2 * RIM
    for j in range(tiles):
        lanes = slice(j * LANES, (j + 1) * LANES)
        for g in range(own // 8):
            water[j, 8 + g * 8:16 + g * 8, :] = water_in[g * 8:g * 8 + 8, lanes].astype(jnp.float32)
        water[j, 8 + own:8 + slots, :] = rims[j, rim_first:rim_first + 8, :]
        water[j, 7:8, :] = water[j, 7 + slots:8 + slots, :]
        water[j, 8 + slots:9 + slots, :] = water[j, 8:9, :]
        for k in range(levels - 1):
            mix[k, j, own:slots, :] = rims[j, rim_first + 8 * (k + 1):rim_first + 8 * (k + 2), :]

    def mask_rows(g, carry):
        base = pl.multiple_of(8 + g * 8, 8)
        here = [water[j, pl.ds(base, 8), :] for j in range(tiles)]
        right = [pltpu.roll(v, LANES - 1, 1) for v in here]
        left = [pltpu.roll(v, 1, 1) for v in here]
        rows = pl.ds(pl.multiple_of(g * 8, 8), 8)
        for j in range(tiles):
            masks[0, j, rows, :] = here[j]
            masks[1, j, rows, :] = here[j] * water[j, pl.ds(base + 1, 8), :]
            masks[2, j, rows, :] = here[j] * water[j, pl.ds(base - 1, 8), :]
            beyond = right[j + 1] if j + 1 < tiles else jnp.zeros_like(lane, jnp.float32)
            before = left[j - 1] if j > 0 else jnp.zeros_like(lane, jnp.float32)
            masks[3, j, rows, :] = here[j] * jnp.where(last, beyond, right[j])
            masks[4, j, rows, :] = here[j] * jnp.where(first, before, left[j])
        return carry

    lax.fori_loop(0, slots // 8, mask_rows, 0)

    def spread_own(row, carry):
        for j in range(tiles):
            lanes = slice(j * LANES, (j + 1) * LANES)
            wet = masks[0, j, pl.ds(row, 1), :]
            for l in range(levels):
                value = strips[j, pl.ds(l * own + row, recv, stride=levels * own), :]
                field[0, l, row, :, lanes] = value
                source[l, row, :, lanes] = wet * value
        return carry

    lax.fori_loop(0, own, spread_own, 0)

    def spread_rim(row, carry):
        for j in range(tiles):
            lanes = slice(j * LANES, (j + 1) * LANES)
            wet = masks[0, j, pl.ds(own + row, 1), :]
            for l in range(levels):
                value = rims[j, pl.ds(l * 2 * RIM + row, recv, stride=levels * 2 * RIM), :]
                field[0, l, own + row, :, lanes] = value
                source[l, own + row, :, lanes] = wet * value
        return carry

    lax.fori_loop(0, 2 * RIM, spread_rim, 0)

    for copy in cur_copies:
        copy.wait()

    keep = keep_ref[...]
    for step in range(HOURS):
        hour = HOURS - 1 - step

        def weigh(i, carry):
            g = lax.rem(i, slots // 8)
            l = i // (slots // 8)
            rows = pl.ds(pl.multiple_of(g * 8, 8), 8)
            for j in range(tiles):
                lanes = slice(j * LANES, (j + 1) * LANES)
                u = cur[l, hour, rows, lanes].astype(jnp.float32)
                v = cur[levels + l, hour, rows, lanes].astype(jnp.float32)
                down = (jnp.maximum(u, 0.0) + diffusion_number) * masks[1, j, rows, :]
                up = (jnp.maximum(-u, 0.0) + diffusion_number) * masks[2, j, rows, :]
                right = (jnp.maximum(v, 0.0) + diffusion_number) * masks[3, j, rows, :]
                left = (jnp.maximum(-v, 0.0) + diffusion_number) * masks[4, j, rows, :]
                weights[0, l, j, rows, :] = masks[0, j, rows, :] - ((down + up) + (right + left))
                weights[1, l, j, rows, :] = down
                weights[2, l, j, rows, :] = up
                weights[3, l, j, rows, :] = right
                weights[4, l, j, rows, :] = left
            return carry

        lax.fori_loop(0, levels * (slots // 8), weigh, 0)

        reach = HOURS - 1 - step
        old, new = step % 2, 1 - step % 2
        obs = obs_ref[hour]
        is_last = step == HOURS - 1

        def advance(i, carry):
            row = i - reach
            at = jnp.where(row < 0, row + slots, row)
            below = jnp.where(at == slots - 1, 0, at + 1)
            above = jnp.where(at == 0, slots - 1, at - 1)
            here = pl.ds(at, 1)
            value = [[None] * levels for _ in range(tiles + 1)]
            turn_r = [[None] * levels for _ in range(tiles + 1)]
            turn_l = [[None] * levels for _ in range(tiles + 1)]

            def fetch(j):
                lanes = slice(j * LANES, (j + 1) * LANES)
                for l in range(levels):
                    v = field[old, l, at, :, lanes]
                    value[j][l] = v
                    turn_r[j][l] = pltpu.roll(v, LANES - 1, 1)
                    turn_l[j][l] = pltpu.roll(v, 1, 1)

            fetch(0)
            for j in range(tiles):
                lanes = slice(j * LANES, (j + 1) * LANES)
                if j + 1 < tiles:
                    fetch(j + 1)
                moved = []
                for l in range(levels):
                    beyond = turn_r[j + 1][l] if j + 1 < tiles else turn_r[j][l]
                    before = turn_l[j - 1][l] if j > 0 else turn_l[j][l]
                    east = jnp.where(last, beyond, turn_r[j][l])
                    west = jnp.where(first, before, turn_l[j][l])
                    acc = weights[0, l, j, here, :] * value[j][l]
                    acc = acc + weights[1, l, j, here, :] * field[old, l, below, :, lanes]
                    acc = acc + weights[2, l, j, here, :] * field[old, l, above, :, lanes]
                    acc = acc + weights[3, l, j, here, :] * east
                    acc = acc + weights[4, l, j, here, :] * west
                    moved.append(acc)
                flux = [mix[k, j, here, :] * (moved[k + 1] - moved[k]) for k in range(levels - 1)]
                for l in range(levels):
                    mixed = moved[l]
                    if l < levels - 1:
                        mixed = mixed + flux[l]
                    if l > 0:
                        mixed = mixed - flux[l - 1]
                    result = keep * mixed + obs * source[l, at, :, lanes]
                    field[new, l, at, :, lanes] = result
                    if is_last:
                        strips[j, pl.ds(l * own + row, recv, stride=levels * own), :] = result
            return carry

        lax.fori_loop(0, own + 2 * reach, advance, 0)

    out_copies = [
        pltpu.make_async_copy(strips.at[j], start_hbm.at[:, pl.ds(j * LANES, LANES)], sem_out)
        for j in range(tiles)
    ]
    for copy in out_copies:
        copy.start()

    final = HOURS % 2

    def tabulate(row, carry):
        for j in range(tiles):
            lanes = slice(j * LANES, (j + 1) * LANES)
            stack = jnp.concatenate([field[final, l, row, :, lanes] for l in range(levels)], axis=0)
            stack = jnp.concatenate([stack] * (LANES // (levels * recv)), axis=0)
            at = pl.multiple_of((row * tiles + j) * LANES, LANES)
            table[pl.ds(at, LANES), :] = stack.T
        return carry

    lax.fori_loop(0, own, tabulate, 0)

    channels = levels * recv
    lane_row = lax.broadcasted_iota(jnp.int32, (1, LANES), 1)
    ways = LANES // channels

    def pick(g, carry):
        for c in range(LANES):
            value = table[pl.ds(cells_ref[g * ways, c], 1), :]
            for q in range(1, ways):
                other = table[pl.ds(cells_ref[g * ways + q, c], 1), :]
                value = jnp.where(lane_row < q * channels, value, other)
            picked[c:c + 1, :] = value
        outgoing[pl.ds(pl.multiple_of(g * LANES, LANES), LANES), :] = picked[...].T
        return carry

    lax.fori_loop(0, cells_ref.shape[0] // ways, pick, 0)
    samples_copy = pltpu.make_async_copy(outgoing, samples_hbm, sem_samples)
    samples_copy.start()
    samples_copy.wait()
    for copy in out_copies:
        copy.wait()


def response_kernel(samples_ref, profiles_ref, out_ref):
    batches, strips, channels, cells = samples_ref.shape
    levels = profiles_ref.shape[2] // cells
    recv = channels // levels
    for s in range(strips):
        total = None
        for l in range(levels):
            left = samples_ref[:, s, l * recv:(l + 1) * recv, :].reshape(batches * recv, cells)
            right = profiles_ref[s, 0, l * cells:(l + 1) * cells, :]
            part = jnp.dot(
                left, right, precision=lax.Precision.HIGHEST, preferred_element_type=jnp.float32
            )
            total = part if total is None else total + part
        out_ref[s, 0] = total


def rims_of(block, dim):
    count = lax.axis_size("space")
    forward = [(i, i + 1) for i in range(count - 1)]
    backward = [(b, a) for a, b in forward]
    size = block.shape[dim]
    low = lax.ppermute(lax.slice_in_dim(block, size - RIM, size, axis=dim), "space", forward)
    high = lax.ppermute(lax.slice_in_dim(block, 0, RIM, axis=dim), "space", backward)
    return jnp.concatenate([high, low], axis=dim)


def on_device(
    adjoint_end, currents, plan, water_mask, mixing, decay, obs_weight, release_cells, profiles
):
    recv, levels, own, width = adjoint_end.shape
    batches = lax.axis_size("rcpt")
    here = lax.axis_index("rcpt")
    x_count = batches // 2

    mine = currents[0]
    extended = jnp.concatenate([mine, rims_of(mine, 2)], axis=2)
    slots = own + 2 * RIM
    pieces = extended.reshape(batches, slots, width)
    pieces = lax.all_to_all(pieces, "rcpt", split_axis=0, concat_axis=0, tiled=True)
    wanted = jnp.take(pieces, plan, axis=0)
    across = [(i, i ^ 1) for i in range(batches)]
    partner = lax.ppermute(wanted, "rcpt", across)
    arrivals = [wanted, partner]
    for dx in range(1, x_count):
        route = [(i, (i - 2 * dx) % batches) for i in range(batches)]
        arrivals.append(lax.ppermute(wanted, "rcpt", route))
        arrivals.append(lax.ppermute(partner, "rcpt", route))

    edges = jnp.concatenate(
        [
            adjoint_end.reshape(recv * levels, own, width),
            water_mask.astype(jnp.float32)[None],
            mixing,
        ],
        axis=0,
    )
    rim = rims_of(edges, 1)
    rim = rim.reshape(-1, width)

    keep = jnp.broadcast_to((1.0 - decay)[:, None], (recv, LANES))
    obs = jnp.broadcast_to(obs_weight[:, :, None], (HOURS, recv, LANES))
    place = jnp.stack([here // 2, here % 2]).astype(jnp.int32)
    tiles = width // LANES
    blocks, cells = release_cells.shape[1:]
    channels = recv * levels
    hbm = pl.BlockSpec(memory_space=pl.ANY)
    smem = pl.BlockSpec(memory_space=pltpu.SMEM)
    vmem = pl.BlockSpec(memory_space=pltpu.VMEM)
    f32 = jnp.float32
    start, samples = pl.pallas_call(
        transport_kernel,
        out_shape=(
            jax.ShapeDtypeStruct((channels * own, width), f32),
            jax.ShapeDtypeStruct((blocks * channels, cells), f32),
        ),
        in_specs=[smem, smem, vmem, vmem] + [hbm] * 12,
        out_specs=(hbm, hbm),
        scratch_shapes=[
            pltpu.VMEM((tiles, channels * own, LANES), f32),
            pltpu.VMEM((tiles, (channels + levels) * 2 * RIM, LANES), f32),
            pltpu.VMEM((2, levels, slots, recv, width), f32),
            pltpu.VMEM((levels, slots, recv, width), f32),
            pltpu.VMEM((own, width), jnp.int32),
            pltpu.VMEM((tiles, slots + 16, LANES), f32),
            pltpu.VMEM((5, tiles, slots, LANES), f32),
            pltpu.VMEM((levels - 1, tiles, slots, LANES), f32),
            pltpu.VMEM((2 * levels, HOURS, slots, width), jnp.bfloat16),
            pltpu.VMEM((5, levels, tiles, slots, LANES), f32),
            pltpu.VMEM((own * width, LANES), f32),
            pltpu.VMEM((cells, LANES), f32),
            pltpu.VMEM((blocks * channels, cells), f32),
        ]
        + [pltpu.SemaphoreType.DMA] * 7,
        compiler_params=pltpu.CompilerParams(vmem_limit_bytes=67_000_000),
        name="transport",
    )(
        place, release_cells[0], keep, obs,
        adjoint_end.reshape(channels * own, width), rim, water_mask, mixing, *arrivals,
    )
    sending = samples.reshape(blocks, channels, cells)
    gathered = lax.all_to_all(sending, ("rcpt", "space"), split_axis=0, concat_axis=0, tiled=True)
    strips = lax.axis_size("space")
    gathered = gathered.reshape(batches, strips, channels, cells)
    group = 4
    own_blocks, depth, scenarios = profiles.shape[1:]
    result = pl.pallas_call(
        response_kernel,
        grid=(strips // group,),
        out_shape=jax.ShapeDtypeStruct((strips, own_blocks, batches * recv, scenarios), f32),
        in_specs=[
            pl.BlockSpec((batches, group, channels, cells), lambda s: (0, s, 0, 0)),
            pl.BlockSpec((group, own_blocks, depth, scenarios), lambda s: (s, 0, 0, 0)),
        ],
        out_specs=pl.BlockSpec((group, own_blocks, batches * recv, scenarios), lambda s: (s, 0, 0, 0)),
        name="response",
    )(gathered, profiles)
    return (start.reshape(recv, levels, own, width), result)


def solution(mesh):
    placed = (
        P("rcpt", None, "space", None),
        P("rcpt", None, None, "space", None),
        P(),
        P("space", None),
        P(None, "space", None),
        P("rcpt"),
        P(None, "rcpt"),
        P("space", None, None),
        P(None, ("rcpt", "space"), None, None),
    )
    return jax.shard_map(
        on_device,
        mesh=mesh,
        in_specs=placed,
        out_specs=(P("rcpt", None, "space", None), P(None, ("rcpt", "space"), None, None)),
        check_vma=False,
    )
```

time: 1300 us -> 186 us (0.14); the launches traced: 1280 us -> 185 us
  local copies, waits for them, and re-layouts: 1040 us -> 3.05 us
  waiting for transfers between devices: 125 us -> 26 us
  Pallas kernels: 0 us -> 76.8 us
  other arithmetic: 58 us -> 7.85 us
  blocking collectives: 0 us -> 41.5 us
  between operations: 17.4 us -> 0.79 us
  starting transfers between devices: 41.9 us -> 28.9 us
    gather x2 -> x1, local copies, waits for them, and re-layouts: 966 us -> 0.57 us  [on_device(): wanted = jnp.take(pieces, plan, axis=0)]
    psum x1 -> x0, waiting for transfers between devices: 101 us -> none  [broadcast(): return lax.psum(kept, axis)]
    pallas_call x0 -> x2, Pallas kernels: none -> 76.8 us  [the longest x1 70.3 us: on_device(): pl.pallas_call(transport_kernel, out_shape=(jax.ShapeDtypeStruct((channel...]
    all_to_all x0 -> x1, blocking collectives: none -> 41.5 us  [on_device(): lax.all_to_all(sending, ('rcpt', 'space'), split_axis=0, concat_axis=0, t...]
    mul x11 -> x0, other arithmetic: 38.3 us -> none  [the longest x4 31.1 us: transport(): moved = moved * inner]
    add x3 -> x0, local copies, waits for them, and re-layouts: 30.6 us -> none  [the longest x1 30.4 us: on_device(): field = keep * mixed + obs_weight[hour_index][:, None, None, None] * source]
    slice x12 -> x1, local copies, waits for them, and re-layouts: 24.5 us -> 1.03 us  [rims_of(): lax.slice_in_dim(block, 0, RIM, axis=dim)]
    ppermute x10 -> x11, waiting for transfers between devices: 0.03 us -> 21.9 us  [the longest x3 12.7 us: on_device(): arrivals.append(lax.ppermute(partner, 'rcpt', route))]
  transfers between devices with their start and end apart: 12 -> 12, of which waited for: 2 -> 8; matrix products, arithmetic and copies ran while one was open for 3% -> 3% of each run, Pallas kernels for 0% -> 0%
where the time goes in v1:
time: 186 us; the launch traced here: 185 us
  Pallas kernels  76.8 us (41%)
  blocking collectives  41.5 us (22%)
  starting transfers between devices  28.9 us (16%)
  waiting for transfers between devices  26 us (14%)
  other arithmetic  7.85 us (4%)
  local copies, waits for them, and re-layouts  3.05 us (2%)
    pallas_call x1, Pallas kernels, on_device(): pl.pallas_call(transport_kernel, out_shape=(jax.ShapeDtypeStruct((channel...  70.3 us
    all_to_all x1, blocking collectives, on_device(): lax.all_to_all(sending, ('rcpt', 'space'), split_axis=0, concat_axis=0, t...  41.5 us
    ppermute x3, waiting for transfers between devices, on_device(): arrivals.append(lax.ppermute(partner, 'rcpt', route))  12.7 us
    ppermute x2, starting transfers between devices, rims_of(): lax.ppermute(lax.slice_in_dim(block, size - RIM, size, axis=dim), 'space'...  7.16 us
    all_to_all x1, starting transfers between devices, on_device(): lax.all_to_all(pieces, 'rcpt', split_axis=0, concat_axis=0, tiled=True)  6.53 us
    pallas_call x1, Pallas kernels, on_device(): pl.pallas_call(response_kernel, grid=(strips // group,), out_shape=jax.Sh...  6.5 us
    ppermute x2, starting transfers between devices, rims_of(): lax.ppermute(lax.slice_in_dim(block, 0, RIM, axis=dim), 'space', backward)  5.21 us
    ppermute x1, waiting for transfers between devices, on_device(): partner = lax.ppermute(wanted, 'rcpt', across)  4.5 us
  transfers between devices with their start and end apart: 12, of which 8 were waited for; matrix products, arithmetic and copies ran while one was open for 3% of the time, Pallas kernels for 0%

profile of v1, /device:TPU:1, one launch (start us, length us, event | category | flops | bytes accessed | tf_op | source)
XLA Modules:
  0.0 185.0 jit_solution(1357897164854858704)
XLA Ops:
  0.6 1.0 fusion
  1.7 3.3 %collective-permute-start.2 = (bf16[2,4,4,1024]{3,2,1,0:T(4,128)(2,1)S(1)}, bf16[2,4,4,1024]{3,2,1,0:T(4,128)(2,1)S(1)}, u32[]{:S(2)}, u32[]{:S(2)}) collective-permute-start(bf16[2,4,4,1024]{3,2,1,0:T(4,128)(2,1)S(1)} %get-tuple-element.8), channel_id=1, source_target_pairs={{1,0},{2,1},{3,2},{4,3},{5,4},{6,5},{7,6},{8,7},{9,8},{10,9},{11,1... | collective-permute-start | bytes 196616 | tf_op jit(solution)/shard_map/ppermute | solution.py:259
  5.0 3.2 %collective-permute-start.3 = (bf16[2,4,4,1024]{3,2,1,0:T(4,128)(2,1)S(1)}, bf16[2,4,4,1024]{3,2,1,0:T(4,128)(2,1)S(1)}, u32[]{:S(2)}, u32[]{:S(2)}) collective-permute-start(bf16[2,4,4,1024]{3,2,1,0:T(4,128)(2,1)S(1)} %get-tuple-element.9), channel_id=1, source_target_pairs={{0,1},{1,2},{2,3},{3,4},{4,5},{5,6},{6,7},{7,8},{8,9},{9,10},{10,1... | collective-permute-start | bytes 196616 | tf_op jit(solution)/shard_map/ppermute | solution.py:258
  8.2 0.9 convert_bitcast_fusion
  9.5 2.0 %pad_maximum_fusion = bf16[8,40,1024]{2,1,0:T(8,128)(2,1)} fusion(bf16[8,4,1024]{2,1,0:T(4,128)(2,1)S(1)} %bitcast.24, bf16[8,4,1024]{2,1,0:T(4,128)(2,1)S(1)} %bitcast.23, bf16[8,32,1024]{2,1,0:T(8,128)(2,1)} %bitcast.21), kind=kLoop, calls=%fused_computation.2 | loop fusion | flops 1966080 | bytes 1310720 | tf_op jit(solution)/shard_map/concatenate | solution.py:272
  11.5 6.5 %all-to-all-start = ((bf16[8,40,1024]{2,1,0:T(8,128)(2,1)}), bf16[8,40,1024]{2,1,0:T(8,128)(2,1)S(1)}, u32[]{:S(2)}, u32[]{:S(2)}) async-start(bf16[8,40,1024]{2,1,0:T(8,128)(2,1)} %pad_maximum_fusion), calls=%async_computation | async-start | bytes 1310720 | tf_op jit(solution)/shard_map/all_to_all | solution.py:275
  18.1 1.8 pad_maximum_fusion.3
  19.9 1.9 %collective-permute-start = (f32[36,4,1024]{2,1,0:T(4,128)S(1)}, f32[36,4,1024]{2,1,0:T(4,128)S(1)}, u32[]{:S(2)}, u32[]{:S(2)}) collective-permute-start(f32[36,4,1024]{2,1,0:T(4,128)S(1)} %get-tuple-element.6), channel_id=1, source_target_pairs={{1,0},{2,1},{3,2},{4,3},{5,4},{6,5},{7,6},{8,7},{9,8},{10,9},{11,1... | collective-permute-start | bytes 1769480 | tf_op jit(solution)/shard_map/ppermute | solution.py:259
  21.8 3.9 %collective-permute-start.1 = (f32[36,4,1024]{2,1,0:T(4,128)S(1)}, f32[36,4,1024]{2,1,0:T(4,128)}, u32[]{:S(2)}, u32[]{:S(2)}) collective-permute-start(f32[36,4,1024]{2,1,0:T(4,128)S(1)} %get-tuple-element.7), channel_id=1, source_target_pairs={{0,1},{1,2},{2,3},{3,4},{4,5},{5,6},{6,7},{7,8},{8,9},{9,10},{10,1... | collective-permute-start | bytes 1769480 | tf_op jit(solution)/shard_map/ppermute | solution.py:258
  25.8 4.1 %all-to-all-done = bf16[8,40,1024]{2,1,0:T(8,128)(2,1)S(1)} async-done(((bf16[8,40,1024]{2,1,0:T(8,128)(2,1)}), bf16[8,40,1024]{2,1,0:T(8,128)(2,1)S(1)}, u32[]{:S(2)}, u32[]{:S(2)}) %all-to-all-start) | async-done | bytes 655392 | tf_op jit(solution)/shard_map/all_to_all | solution.py:275
  30.7 2.6 %collective-permute-start.4 = (bf16[4,40,1024]{2,1,0:T(8,128)(2,1)S(1)}, bf16[4,40,1024]{2,1,0:T(8,128)(2,1)S(1)}, u32[]{:S(2)}, u32[]{:S(2)}) collective-permute-start(bf16[4,40,1024]{2,1,0:T(8,128)(2,1)S(1)} %broadcast_select_fusion.p0), channel_id=1, source_target_pairs={{0,16},{16,0},{32,48},{48,32},{64,80},{80,64},{96,112},{112,96},{1... | collective-permute-start | bytes 983048 | tf_op jit(solution)/shard_map/ppermute | solution.py:278
  34.1 1.2 collective-permute-start.7
  35.3 2.9 %collective-permute-done = f32[36,4,1024]{2,1,0:T(4,128)S(1)} collective-permute-done((f32[36,4,1024]{2,1,0:T(4,128)S(1)}, f32[36,4,1024]{2,1,0:T(4,128)S(1)}, u32[]{:S(2)}, u32[]{:S(2)}) %collective-permute-start) | collective-permute-done | bytes 589856 | tf_op jit(solution)/shard_map/ppermute | solution.py:259
  38.2 1.5 collective-permute-start.5
  39.7 4.5 %collective-permute-done.4.p1 = bf16[4,40,1024]{2,1,0:T(8,128)(2,1)S(1)} collective-permute-done((bf16[4,40,1024]{2,1,0:T(8,128)(2,1)S(1)}, bf16[4,40,1024]{2,1,0:T(8,128)(2,1)S(1)}, u32[]{:S(2)}, u32[]{:S(2)}) %collective-permute-start.4) | collective-permute-done | bytes 327712 | tf_op jit(solution)/shard_map/ppermute | solution.py:278
  45.1 2.7 %collective-permute-start.8 = (bf16[4,40,1024]{2,1,0:T(8,128)(2,1)S(1)}, bf16[4,40,1024]{2,1,0:T(8,128)(2,1)S(1)}, u32[]{:S(2)}, u32[]{:S(2)}) collective-permute-start(bf16[4,40,1024]{2,1,0:T(8,128)(2,1)S(1)} %collective-permute-done.4.p1), channel_id=1, source_target_pairs={{0,64},{16,80},{32,96},{48,112},{64,0},{80,16},{96,32},{112,48},{1... | collective-permute-start | bytes 983048 | tf_op jit(solution)/shard_map/ppermute | solution.py:283
  48.7 2.4 %maximum_bitcast_fusion.rim_hbm = f32[288,1024]{1,0:T(8,128)} fusion(f32[36,4,1024]{2,1,0:T(4,128)} %collective-permute-done.1, f32[36,4,1024]{2,1,0:T(4,128)S(1)} %collective-permute-done), kind=kLoop, calls=%fused_computation.1 | loop fusion | flops 294912 | bytes 2359296 | tf_op jit(solution)/shard_map/reshape | solution.py:294
  51.1 1.5 collective-permute-done.5.p2
  52.6 5.6 %collective-permute-done.10.p7 = bf16[4,40,1024]{2,1,0:T(8,128)(2,1)S(1)} collective-permute-done((bf16[4,40,1024]{2,1,0:T(8,128)(2,1)S(1)}, bf16[4,40,1024]{2,1,0:T(8,128)(2,1)S(1)}, u32[]{:S(2)}, u32[]{:S(2)}) %collective-permute-start.10) | collective-permute-done | bytes 327712 | tf_op jit(solution)/shard_map/ppermute | solution.py:283
  58.2 4.9 %collective-permute-done.8.p5 = bf16[4,40,1024]{2,1,0:T(8,128)(2,1)S(1)} collective-permute-done((bf16[4,40,1024]{2,1,0:T(8,128)(2,1)S(1)}, bf16[4,40,1024]{2,1,0:T(8,128)(2,1)S(1)}, u32[]{:S(2)}, u32[]{:S(2)}) %collective-permute-start.8) | collective-permute-done | bytes 327712 | tf_op jit(solution)/shard_map/ppermute | solution.py:283
  63.1 2.1 %collective-permute-done.6.p3 = bf16[4,40,1024]{2,1,0:T(8,128)(2,1)S(1)} collective-permute-done((bf16[4,40,1024]{2,1,0:T(8,128)(2,1)S(1)}, bf16[4,40,1024]{2,1,0:T(8,128)(2,1)S(1)}, u32[]{:S(2)}, u32[]{:S(2)}) %collective-permute-start.6) | collective-permute-done | bytes 327712 | tf_op jit(solution)/shard_map/ppermute | solution.py:283
  66.7 70.3 %transport.1 = (f32[1024,1024]{1,0:T(8,128)}, f32[4096,128]{1,0:T(8,128)}) custom-call(s32[2]{0:T(128)} %pad_add_fusion.where_ref, s32[128,128]{1,0:T(8,128)} %bitcast.22, f32[8,128]{1,0:T(8,128)} %broadcast_in_dim.27.keep_ref, f32[4,8,128]{2,1,0:T(8,128)} %broadcast_in_dim.28.obs_ref, f32[1024,1024]{1,0:T(8,128)} %bitcast.17, ...), custom_call_target="tpu_custom_call" | custom-call | tf_op jit(solution)/shard_map/transport/pallas_call | solution.py:306
  137.0 41.5 %all_to_all.10 = f32[128,32,128]{2,1,0:T(8,128)} all-to-all(f32[128,32,128]{2,1,0:T(8,128)} %bitcast.19), channel_id=1, replica_groups=mesh['rcpt'=8,'space'=16] {'rcpt','space'}, dimensions={0} | all-to-all | bytes 4194304 | tf_op jit(solution)/shard_map/all_to_all | solution.py:337
  178.5 6.5 %response.1 = f32[16,1,64,128]{3,2,1,0:T(8,128)} custom-call(f32[8,16,32,128]{3,2,1,0:T(8,128)} %bitcast.18, f32[16,1,512,128]{3,2,1,0:T(8,128)} %profiles_ref.1), custom_call_target="tpu_custom_call" | custom-call | tf_op jit(solution)/shard_map/response/pallas_call | solution.py:342
  (41 shorter events, 5.2 us)
Async XLA Ops:
  1.7 7.4 %collective-permute-start.2 = (bf16[2,4,4,1024]{3,2,1,0:T(4,128)(2,1)S(1)}, bf16[2,4,4,1024]{3,2,1,0:T(4,128)(2,1)S(1)}, u32[]{:S(2)}, u32[]{:S(2)}) collective-permute-start(bf16[2,4,4,1024]{3,2,1,0:T(4,128)(2,1)S(1)} %get-tuple-element.8), channel_id=1, source_target_pairs={{1,0},{2,1},{3,2},{4,3},{5,4},{6,5},{7,6},{8,7},{9,8},{10,9},{11,1... | collective-permute-start | bytes 196616 | tf_op jit(solution)/shard_map/ppermute | solution.py:259
  5.0 4.5 %collective-permute-start.3 = (bf16[2,4,4,1024]{3,2,1,0:T(4,128)(2,1)S(1)}, bf16[2,4,4,1024]{3,2,1,0:T(4,128)(2,1)S(1)}, u32[]{:S(2)}, u32[]{:S(2)}) collective-permute-start(bf16[2,4,4,1024]{3,2,1,0:T(4,128)(2,1)S(1)} %get-tuple-element.9), channel_id=1, source_target_pairs={{0,1},{1,2},{2,3},{3,4},{4,5},{5,6},{6,7},{7,8},{8,9},{9,10},{10,1... | collective-permute-start | bytes 196616 | tf_op jit(solution)/shard_map/ppermute | solution.py:258
  9.5 8.6 %copy-start = (f32[3,32,1024]{2,1,0:T(8,128)S(1)}, f32[3,32,1024]{2,1,0:T(8,128)}, u32[]{:S(2)}) copy-start(f32[3,32,1024]{2,1,0:T(8,128)} %mix_hbm.1) | copy-start | bytes 1179652
  11.5 18.4 %all-to-all-start = ((bf16[8,40,1024]{2,1,0:T(8,128)(2,1)}), bf16[8,40,1024]{2,1,0:T(8,128)(2,1)S(1)}, u32[]{:S(2)}, u32[]{:S(2)}) async-start(bf16[8,40,1024]{2,1,0:T(8,128)(2,1)} %pad_maximum_fusion), calls=%async_computation | async-start | bytes 1310720 | tf_op jit(solution)/shard_map/all_to_all | solution.py:275
  18.1 7.7 %copy-start.10 = (s32[4]{0:T(128)S(1)}, s32[4]{0:T(128)}, u32[]{:S(2)}) copy-start(s32[4]{0:T(128)} %param.11) | copy-start | bytes 52
  19.9 28.8 %copy-start.11 = (f32[8]{0:T(128)S(1)}, f32[8]{0:T(128)}, u32[]{:S(2)}) copy-start(f32[8]{0:T(128)} %param.14) | copy-start | bytes 100
  19.9 18.3 %collective-permute-start = (f32[36,4,1024]{2,1,0:T(4,128)S(1)}, f32[36,4,1024]{2,1,0:T(4,128)S(1)}, u32[]{:S(2)}, u32[]{:S(2)}) collective-permute-start(f32[36,4,1024]{2,1,0:T(4,128)S(1)} %get-tuple-element.6), channel_id=1, source_target_pairs={{1,0},{2,1},{3,2},{4,3},{5,4},{6,5},{7,6},{8,7},{9,8},{10,9},{11,1... | collective-permute-start | bytes 1769480 | tf_op jit(solution)/shard_map/ppermute | solution.py:259
  21.8 23.3 %collective-permute-start.1 = (f32[36,4,1024]{2,1,0:T(4,128)S(1)}, f32[36,4,1024]{2,1,0:T(4,128)}, u32[]{:S(2)}, u32[]{:S(2)}) collective-permute-start(f32[36,4,1024]{2,1,0:T(4,128)S(1)} %get-tuple-element.7), channel_id=1, source_target_pairs={{0,1},{1,2},{2,3},{3,4},{4,5},{5,6},{6,7},{7,8},{8,9},{9,10},{10,1... | collective-permute-start | bytes 1769480 | tf_op jit(solution)/shard_map/ppermute | solution.py:258
  30.6 7.5 %copy-start.1 = (bf16[4,40,1024]{2,1,0:T(8,128)(2,1)}, bf16[4,40,1024]{2,1,0:T(8,128)(2,1)S(1)}, u32[]{:S(2)}) copy-start(bf16[4,40,1024]{2,1,0:T(8,128)(2,1)S(1)} %broadcast_select_fusion.p0) | copy-start | bytes 983044
  30.7 35.3 %copy-start.9 = (f32[4,8]{1,0:T(4,128)S(1)}, f32[4,8]{1,0:T(4,128)}, u32[]{:S(2)}) copy-start(f32[4,8]{1,0:T(4,128)} %param.15) | copy-start | bytes 388
  30.7 13.5 %collective-permute-start.4 = (bf16[4,40,1024]{2,1,0:T(8,128)(2,1)S(1)}, bf16[4,40,1024]{2,1,0:T(8,128)(2,1)S(1)}, u32[]{:S(2)}, u32[]{:S(2)}) collective-permute-start(bf16[4,40,1024]{2,1,0:T(8,128)(2,1)S(1)} %broadcast_select_fusion.p0), channel_id=1, source_target_pairs={{0,16},{16,0},{32,48},{48,32},{64,80},{80,64},{96,112},{112,96},{1... | collective-permute-start | bytes 983048 | tf_op jit(solution)/shard_map/ppermute | solution.py:278
  33.2 14.6 %collective-permute-start.9 = (bf16[4,40,1024]{2,1,0:T(8,128)(2,1)S(1)}, bf16[4,40,1024]{2,1,0:T(8,128)(2,1)S(1)}, u32[]{:S(2)}, u32[]{:S(2)}) collective-permute-start(bf16[4,40,1024]{2,1,0:T(8,128)(2,1)S(1)} %broadcast_select_fusion.p0), channel_id=1, source_target_pairs={{0,32},{16,48},{32,64},{48,80},{64,96},{80,112},{96,0},{112,16},{1... | collective-permute-start | bytes 983048 | tf_op jit(solution)/shard_map/ppermute | solution.py:282
  34.1 17.0 %collective-permute-start.7 = (bf16[4,40,1024]{2,1,0:T(8,128)(2,1)S(1)}, bf16[4,40,1024]{2,1,0:T(8,128)(2,1)S(1)}, u32[]{:S(2)}, u32[]{:S(2)}) collective-permute-start(bf16[4,40,1024]{2,1,0:T(8,128)(2,1)S(1)} %broadcast_select_fusion.p0), channel_id=1, source_target_pairs={{0,64},{16,80},{32,96},{48,112},{64,0},{80,16},{96,32},{112,48},{1... | collective-permute-start | bytes 983048 | tf_op jit(solution)/shard_map/ppermute | solution.py:282
  38.2 14.4 %collective-permute-start.5 = (bf16[4,40,1024]{2,1,0:T(8,128)(2,1)S(1)}, bf16[4,40,1024]{2,1,0:T(8,128)(2,1)S(1)}, u32[]{:S(2)}, u32[]{:S(2)}) collective-permute-start(bf16[4,40,1024]{2,1,0:T(8,128)(2,1)S(1)} %broadcast_select_fusion.p0), channel_id=1, source_target_pairs={{0,96},{16,112},{32,0},{48,16},{64,32},{80,48},{96,64},{112,80},{1... | collective-permute-start | bytes 983048 | tf_op jit(solution)/shard_map/ppermute | solution.py:282
  44.2 8.3 %copy-start.2 = (bf16[4,40,1024]{2,1,0:T(8,128)(2,1)}, bf16[4,40,1024]{2,1,0:T(8,128)(2,1)S(1)}, u32[]{:S(2)}) copy-start(bf16[4,40,1024]{2,1,0:T(8,128)(2,1)S(1)} %collective-permute-done.4.p1) | copy-start | bytes 983044
  44.2 14.0 %collective-permute-start.10 = (bf16[4,40,1024]{2,1,0:T(8,128)(2,1)S(1)}, bf16[4,40,1024]{2,1,0:T(8,128)(2,1)S(1)}, u32[]{:S(2)}, u32[]{:S(2)}) collective-permute-start(bf16[4,40,1024]{2,1,0:T(8,128)(2,1)S(1)} %collective-permute-done.4.p1), channel_id=1, source_target_pairs={{0,32},{16,48},{32,64},{48,80},{64,96},{80,112},{96,0},{112,16},{1... | collective-permute-start | bytes 983048 | tf_op jit(solution)/shard_map/ppermute | solution.py:283
  45.1 18.0 %collective-permute-start.8 = (bf16[4,40,1024]{2,1,0:T(8,128)(2,1)S(1)}, bf16[4,40,1024]{2,1,0:T(8,128)(2,1)S(1)}, u32[]{:S(2)}, u32[]{:S(2)}) collective-permute-start(bf16[4,40,1024]{2,1,0:T(8,128)(2,1)S(1)} %collective-permute-done.4.p1), channel_id=1, source_target_pairs={{0,64},{16,80},{32,96},{48,112},{64,0},{80,16},{96,32},{112,48},{1... | collective-permute-start | bytes 983048 | tf_op jit(solution)/shard_map/ppermute | solution.py:283
  47.8 17.4 %copy-start.3 = (bf16[4,40,1024]{2,1,0:T(8,128)(2,1)}, bf16[4,40,1024]{2,1,0:T(8,128)(2,1)S(1)}, u32[]{:S(2)}) copy-start(bf16[4,40,1024]{2,1,0:T(8,128)(2,1)S(1)} %collective-permute-done.9.p6) | copy-start | bytes 983044
  47.8 17.4 %collective-permute-start.6 = (bf16[4,40,1024]{2,1,0:T(8,128)(2,1)S(1)}, bf16[4,40,1024]{2,1,0:T(8,128)(2,1)S(1)}, u32[]{:S(2)}, u32[]{:S(2)}) collective-permute-start(bf16[4,40,1024]{2,1,0:T(8,128)(2,1)S(1)} %collective-permute-done.4.p1), channel_id=1, source_target_pairs={{0,96},{16,112},{32,0},{48,16},{64,32},{80,48},{96,64},{112,80},{1... | collective-permute-start | bytes 983048 | tf_op jit(solution)/shard_map/ppermute | solution.py:283
  51.1 14.2 %copy-start.4 = (bf16[4,40,1024]{2,1,0:T(8,128)(2,1)}, bf16[4,40,1024]{2,1,0:T(8,128)(2,1)S(1)}, u32[]{:S(2)}) copy-start(bf16[4,40,1024]{2,1,0:T(8,128)(2,1)S(1)} %collective-permute-done.7.p4) | copy-start | bytes 983044
  52.6 12.7 %copy-start.5 = (bf16[4,40,1024]{2,1,0:T(8,128)(2,1)}, bf16[4,40,1024]{2,1,0:T(8,128)(2,1)S(1)}, u32[]{:S(2)}) copy-start(bf16[4,40,1024]{2,1,0:T(8,128)(2,1)S(1)} %collective-permute-done.5.p2) | copy-start | bytes 983044
  58.2 7.8 %copy-start.6 = (bf16[4,40,1024]{2,1,0:T(8,128)(2,1)}, bf16[4,40,1024]{2,1,0:T(8,128)(2,1)S(1)}, u32[]{:S(2)}) copy-start(bf16[4,40,1024]{2,1,0:T(8,128)(2,1)S(1)} %collective-permute-done.10.p7) | copy-start | bytes 983044
  63.1 2.9 %copy-start.7 = (bf16[4,40,1024]{2,1,0:T(8,128)(2,1)}, bf16[4,40,1024]{2,1,0:T(8,128)(2,1)S(1)}, u32[]{:S(2)}) copy-start(bf16[4,40,1024]{2,1,0:T(8,128)(2,1)S(1)} %collective-permute-done.8.p5) | copy-start | bytes 983044
  65.2 0.8 copy-start.8
